TPU v7x, 512 devices: a whole 4x8x8 slice. The times are simulated.
512 devices in a mesh: head: 8 (over z), tok: 64 (over x, y, core).
Axes of the slice: x: 4, y: 8, z: 8, core: 2. Of those that a mesh axis runs over, the one named last changes fastest.
Arguments:
- patches: bfloat16 [32768, 1280], P('tok')
- row_table: bfloat16 [64, 1280], replicated, may hold values from -0.59765625 to 0.59765625
- col_table: bfloat16 [64, 1280], replicated, may hold values from -0.59765625 to 0.59765625
- qkv_weight: bfloat16 [3, 1280, 1280], P(None, 'head'), may hold values from -0.15625 to 0.15625
- out_weight: bfloat16 [1280, 1280], P('head'), may hold values from -0.15625 to 0.15625
- merge_weight: bfloat16 [1280, 5120], P('head'), may hold values from -0.078125 to 0.078125
- segment_ids: int32 [32768], P('tok'), may hold values from 0 to 63, as said below
- image_grids: int32 [64, 2], replicated, may hold values from 2 to 62, as said below
- image_offsets: int32 [64], replicated, may hold values from 0 to 32736, as said below
- owners: int32 [64], replicated, may hold values from 0 to 63, each once
Outputs:
- delivered: bfloat16 [15872, 1280], P('tok', 'head')
Inputs may be any that keep to these rules, and one draw needn't show every extreme that they name: `segment_ids`: tokens of each image are consecutive and images follow in order; the pair p of token blocks (tokens 2 * p * 512 to 2 * (p + 1) * 512 - 1) holds exactly images 2 * p and 2 * p + 1, with no padding. `image_grids`: heights are even, widths are 16, and height times width is the image's token count. Within an image each 2x2 window of patches is four consecutive tokens (top left, top right, bottom left, bottom right), windows in row-major order. The longest image has exactly 992 tokens. `image_offsets`: the first token of each image, consistent with segment_ids. `owners`: every device index along tok owns exactly one image.
All inputs are finite; a program needn't handle non-finite values.
Results may differ from a plain program's by a relative error of at most 0.019.
Values may be sent and summed in bfloat16 or wider, within the bound.
No kernel may reach another device: no remote copies, remote signals or barrier semaphores. Data moves between devices by JAX's collectives and lax.ppermute only.
A program may use at most 64 MiB of HBM per device.

v0:
```python
import math
import jax
import jax.numpy as jnp
from jax import lax
from jax.sharding import PartitionSpec as P

HEAD_DIM = 80
CAP = 248


def partner(x, axis, apart):
    return lax.ppermute(x, axis, [(i, i ^ 1 << apart) for i in range(lax.axis_size(axis))])


def layer_norm(values):
    centered = values - jnp.mean(values, axis=-1, keepdims=True)
    variance = jnp.mean(centered * centered, axis=-1, keepdims=True)
    return centered * lax.rsqrt(variance + 1e-06)


def grid_place(token_pos, start_tok, width_now):
    local_pos = token_pos - start_tok
    window = local_pos // 4
    quarter = local_pos % 4
    half_width = jnp.maximum(width_now // 2, 1)
    row_index = 2 * (window // half_width) + quarter // 2
    col_index = 2 * (window % half_width) + quarter % 2
    return (row_index, col_index)


def dot_last(left, right):
    return lax.dot_general(
        left, right, (((1,), (1,)), ((), ())), preferred_element_type=jnp.float32
    )


def on_device(
    patches,
    row_table,
    col_table,
    qkv_weight,
    out_weight,
    merge_weight,
    segment_ids,
    image_grids,
    image_offsets,
    owners,
):
    full_weight = lax.all_gather(out_weight, "head", axis=0, tiled=True)
    block_rows = patches.shape[0]
    width_here = qkv_weight.shape[1]
    heads_here = width_here // HEAD_DIM
    image_count = owners.shape[0]
    image_ids = jnp.arange(image_count, dtype=jnp.int32)
    token_pos = lax.axis_index("tok") * block_rows + jnp.arange(block_rows, dtype=jnp.int32)
    member = segment_ids[:, None] == image_ids[None, :]
    start_tok = jnp.sum(jnp.where(member, image_offsets[None, :], 0), axis=1)
    width_now = jnp.sum(jnp.where(member, image_grids[None, :, 1], 0), axis=1)
    row_index, col_index = grid_place(token_pos, start_tok, width_now)
    side_ids = jnp.arange(row_table.shape[0], dtype=jnp.int32)
    row_onehot = (row_index[:, None] == side_ids[None, :]).astype(jnp.bfloat16)
    col_onehot = (col_index[:, None] == side_ids[None, :]).astype(jnp.bfloat16)
    resid = (
        patches.astype(jnp.float32)
        + jnp.dot(row_onehot, row_table, preferred_element_type=jnp.float32)
        + jnp.dot(col_onehot, col_table, preferred_element_type=jnp.float32)
    )
    normed = layer_norm(resid).astype(jnp.bfloat16)
    query_rows = dot_last(normed, qkv_weight[0]).astype(jnp.bfloat16)
    key_rows = dot_last(normed, qkv_weight[1]).astype(jnp.bfloat16)
    value_rows = dot_last(normed, qkv_weight[2]).astype(jnp.bfloat16)
    seg_wire = segment_ids.astype(jnp.bfloat16)
    far_keys, far_values, far_seg = partner((key_rows, value_rows, seg_wire), "tok", 0)
    query_heads = query_rows.reshape(block_rows, heads_here, HEAD_DIM)
    key_heads = jnp.concatenate([key_rows, far_keys], axis=0).reshape(
        2 * block_rows, heads_here, HEAD_DIM
    )
    value_heads = jnp.concatenate([value_rows, far_values], axis=0).reshape(
        2 * block_rows, heads_here, HEAD_DIM
    )
    query_seg = seg_wire.astype(jnp.float32)
    key_seg = jnp.concatenate([seg_wire, far_seg], axis=0).astype(jnp.float32)
    scores = jnp.einsum(
        "qhd,khd->hqk", query_heads, key_heads, preferred_element_type=jnp.float32
    ) * (1.0 / math.sqrt(HEAD_DIM))
    same_image = query_seg[:, None] == key_seg[None, :]
    raw_weights = jnp.where(same_image[None], jnp.exp(scores), 0.0)
    weight_sum = jnp.sum(raw_weights, axis=-1, keepdims=True)
    attn_probs = (raw_weights / weight_sum).astype(jnp.bfloat16)
    mixed = jnp.einsum("hqk,khd->qhd", attn_probs, value_heads, preferred_element_type=jnp.float32)
    attended = mixed.reshape(block_rows, width_here).astype(jnp.bfloat16)
    group = lax.axis_size("head")
    sent = jnp.broadcast_to(attended[None], (group,) + attended.shape)
    gathered = lax.all_to_all(sent, "head", 0, 0, tiled=True)
    head_total = jnp.einsum(
        "ztf,zfd->td",
        gathered,
        full_weight.reshape(group, width_here, -1),
        preferred_element_type=jnp.float32,
    )
    normed_two = layer_norm(resid + head_total).astype(jnp.bfloat16)
    merged = normed_two.reshape(block_rows // 4, 4 * normed_two.shape[1])
    projected = dot_last(merged, merge_weight).astype(jnp.bfloat16)
    places = lax.axis_size("tok")
    rows_here = projected.shape[0]
    share = rows_here // places
    spread = lax.all_to_all(projected.reshape(places, share, width_here), "tok", 0, 0, tiled=True)
    pair_ids = jnp.arange(places // 2, dtype=jnp.int32)
    place_ids = jnp.arange(places, dtype=jnp.int32)
    wanted = (owners.reshape(-1, 2)[None, :, :] == place_ids[:, None, None]).any(axis=2)
    pieces = jnp.dot(
        wanted.astype(jnp.bfloat16),
        spread.reshape(places // 2, 2 * share * width_here),
        preferred_element_type=jnp.float32,
    ).astype(jnp.bfloat16)
    pair_rows = lax.all_to_all(
        pieces.reshape(places, 2 * share, width_here), "tok", 0, 0, tiled=True
    ).reshape(2 * rows_here, width_here)
    owner_mask = owners == lax.axis_index("tok")
    image_id = jnp.sum(jnp.where(owner_mask, image_ids, 0))
    first_row = (
        jnp.sum(jnp.where(owner_mask, image_offsets, 0)) // 4 - image_id // 2 * 2 * rows_here
    )
    merged_count = jnp.sum(jnp.where(owner_mask, image_grids[:, 0] * image_grids[:, 1], 0)) // 4
    slot_ids = jnp.arange(CAP, dtype=jnp.int32)
    got_ids = jnp.arange(2 * rows_here, dtype=jnp.int32)
    row_of = got_ids // share % 2 * rows_here + got_ids // (2 * share) * share + got_ids % share
    slot_of = row_of - first_row
    selector = (slot_of[None, :] == slot_ids[:, None]) & (slot_ids < merged_count)[:, None]
    owner_rows = jnp.dot(
        selector.astype(jnp.bfloat16), pair_rows, preferred_element_type=jnp.float32
    )
    return owner_rows.astype(jnp.bfloat16)


def solution(mesh):
    placed = (
        P("tok", None),
        P(),
        P(),
        P(None, "head", None),
        P("head", None),
        P("head", None),
        P("tok"),
        P(),
        P(),
        P(),
    )
    return jax.shard_map(
        on_device, mesh=mesh, in_specs=placed, out_specs=P("tok", "head"), check_vma=False
    )
```

profile of v0, /device:TPU:1, one launch (start us, length us, event | category | flops | bytes accessed | tf_op | source)
XLA Modules:
  0.0 146.8 jit_solution(14957617930545872145)
XLA Ops:
  6.5 0.0 copy-start
  6.5 0.0 copy-start.2
  6.5 0.0 all-gather.2.cloned.1.call-start
  6.5 0.7 all-gather.2.cloned.1.call-update
  7.3 0.7 slice_bitcast_fusion
  7.9 0.8 select_reduce_fusion
  8.7 0.1 fusion.22
  8.9 2.0 %convolution_add_fusion.1 = f32[512,1280]{1,0:T(8,128)S(1)} fusion(bf16[64,1280]{1,0:T(8,128)(2,1)} %param.11, bf16[512,1280]{1,0:T(8,128)(2,1)} %param.10, s32[512]{0:T(512)S(1)} %get-tuple-element.13), kind=kOutput, calls=%fused_computation.3 | convolution fusion | flops 85229568 | bytes 4098048 | tf_op jit(solution)/shard_map/dot_general | solution.py:65
  10.9 0.0 copy-done.2
  10.9 0.6 fusion.41
  11.5 0.0 copy-start.1
  11.5 0.4 multiply_reduce_fusion.1
  11.9 0.0 copy-start.7
  11.9 0.0 copy-start.3
  12.0 0.3 multiply_convert_fusion.1
  12.3 0.8 copy-done.1
  13.0 0.7 copy-done.7
  13.7 0.6 convolution_convert_fusion
  14.3 8.8 %collective-permute-start.2 = (bf16[512,160]{0,1:T(8,128)(2,1)S(1)}, bf16[512,160]{0,1:T(8,128)(2,1)S(1)}, u32[]{:S(2)}, u32[]{:S(2)}) collective-permute-start(bf16[512,160]{0,1:T(8,128)(2,1)S(1)} %convolution_convert_fusion), channel_id=1, source_target_pairs={{0,1},{1,0},{2,3},{3,2},{4,5},{5,4},{6,7},{7,6},{8,9},{9,8},{10,11... | collective-permute-start | bytes 491528 | tf_op jit(solution)/shard_map/ppermute | solution.py:12
  23.1 0.0 copy-done.3
  23.1 1.9 %collective-permute-start.1 = (bf16[512]{0:T(512)(128)(2,1)S(1)}, bf16[512]{0:T(512)(128)(2,1)S(1)}, u32[]{:S(2)}, u32[]{:S(2)}) collective-permute-start(bf16[512]{0:T(512)(128)(2,1)S(1)} %get-tuple-element.11), channel_id=1, source_target_pairs={{0,1},{1,0},{2,3},{3,2},{4,5},{5,4},{6,7},{7,6},{8,9},{9,8},{10,11... | collective-permute-start | bytes 3080 | tf_op jit(solution)/shard_map/ppermute | solution.py:12
  25.0 0.6 convolution_convert_fusion.2
  25.6 2.4 %collective-permute-start = (bf16[512,160]{0,1:T(8,128)(2,1)S(1)}, bf16[512,160]{0,1:T(8,128)(2,1)S(1)}, u32[]{:S(2)}, u32[]{:S(2)}) collective-permute-start(bf16[512,160]{0,1:T(8,128)(2,1)S(1)} %convolution_convert_fusion.2), channel_id=1, source_target_pairs={{0,1},{1,0},{2,3},{3,2},{4,5},{5,4},{6,7},{7,6},{8,9},{9,8},{10,11... | collective-permute-start | bytes 491528 | tf_op jit(solution)/shard_map/ppermute | solution.py:12
  28.0 0.6 convolution_convert_fusion.1
  28.6 0.0 collective-permute-done.1
  28.6 0.4 broadcast_compare_fusion
  29.0 0.0 collective-permute-done.2
  29.1 0.0 collective-permute-done
  29.1 1.5 %fusion = (f32[2,512]{1,0:T(2,128)S(1)}, f32[2,512,1024]{2,1,0:T(8,128)S(1)}) fusion(pred[512,1024]{1,0:T(8,128)(4,1)S(1)} %broadcast_compare_fusion, bf16[512,2,80]{0,2,1:T(8,128)(2,1)S(1)} %bitcast.49, bf16[1024,2,80]{0,2,1:T(8,128)(2,1)S(1)} %bitcast.46), kind=kOutput, calls=%fused_computation.4 | convolution fusion | flops 170916864 | bytes 5214208 | tf_op jit(solution)/shard_map/qhd,khd->hqk/dot_general | solution.py:83
  30.6 1.4 fusion.3
  31.9 0.0 copy-start.5
  32.0 0.0 copy-start.4
  32.0 0.0 copy-start.6
  32.0 1.2 broadcast_in_dim.69
  33.2 4.7 %all-to-all-start = ((bf16[8,512,160]{1,2,0:T(8,128)(2,1)}), bf16[8,512,160]{1,2,0:T(8,128)(2,1)S(1)}, u32[]{:S(2)}, u32[]{:S(2)}) async-start(bf16[8,512,160]{1,2,0:T(8,128)(2,1)} %broadcast_in_dim.69), calls=%async_computation | async-start | bytes 2621440 | tf_op jit(solution)/shard_map/all_to_all | solution.py:94
  37.8 0.0 copy-done.5
  37.8 0.1 eq.109
  37.9 0.0 copy-done.4
  38.0 0.0 copy-done.6
  38.0 0.7 fusion.37
  40.0 0.1 copy.12
  41.4 44.9 %all-to-all-done = bf16[8,512,160]{1,2,0:T(8,128)(2,1)S(1)} async-done(((bf16[8,512,160]{1,2,0:T(8,128)(2,1)}), bf16[8,512,160]{1,2,0:T(8,128)(2,1)S(1)}, u32[]{:S(2)}, u32[]{:S(2)}) %all-to-all-start) | async-done | bytes 1310752 | tf_op jit(solution)/shard_map/all_to_all | solution.py:94
  86.3 6.4 %all-gather.2.cloned.1.call-done = bf16[1280,1280]{1,0:T(8,128)(2,1)} async-done(((bf16[160,1280]{1,0:T(8,128)(2,1)}), bf16[1280,1280]{1,0:T(8,128)(2,1)}) %all-gather.2.cloned.1.call-update) | async-done | bytes 3276816 | tf_op jit(solution)/shard_map/all_gather | solution.py:49
  92.7 4.8 %fusion.42 = (f32[512]{0:T(512)S(1)}, f32[512,1280]{1,0:T(8,128)S(1)}) fusion(f32[512,1280]{1,0:T(8,128)} %copy-done.1, bf16[8,512,160]{1,2,0:T(8,128)(2,1)S(1)} %all-to-all-done, bf16[8,160,1280]{2,1,0:T(8,128)(2,1)} %bitcast.45), kind=kOutput, calls=%fused_computation.113 | convolution fusion | flops 1679031808 | bytes 9832448 | tf_op jit(solution)/shard_map/ztf,zfd->td/dot_general | solution.py:95
  97.5 0.4 multiply_reduce_fusion
  98.0 0.3 multiply_convert_fusion
  98.3 1.7 %reshape.260 = bf16[128,5120]{1,0:T(8,128)(2,1)} reshape(bf16[512,1280]{1,0:T(8,128)(2,1)S(1)} %multiply_convert_fusion) | data formatting | bytes 2621440 | tf_op jit(solution)/shard_map/reshape | solution.py:102
  100.0 0.0 copy-done
  100.0 1.9 %convolution_convert_fusion.5 = bf16[128,160]{0,1:T(8,128)(2,1)S(1)} fusion(bf16[128,5120]{1,0:T(8,128)(2,1)} %reshape.260, bf16[160,5120]{1,0:T(8,128)(2,1)S(1)} %copy-done), kind=kOutput, calls=%fused_computation.18 | convolution fusion | flops 209735680 | bytes 2990080 | tf_op jit(solution)/shard_map/dot_general | solution.py:32
  101.9 0.1 copy.13
  102.0 0.7 reshape.261
  102.7 10.4 %all-to-all-start.1 = ((bf16[64,2,160]{2,1,0:T(2,128)(2,1)}), bf16[64,2,160]{2,1,0:T(2,128)(2,1)S(1)}, u32[]{:S(2)}, u32[]{:S(2)}) async-start(bf16[64,2,160]{2,1,0:T(2,128)(2,1)} %reshape.261), calls=%async_computation.1 | async-start | bytes 131072 | tf_op jit(solution)/shard_map/all_to_all | solution.py:107
  113.1 0.1 fusion.16
  113.2 9.7 %all-to-all-done.1 = bf16[64,2,160]{2,1,0:T(2,128)(2,1)S(1)} async-done(((bf16[64,2,160]{2,1,0:T(2,128)(2,1)}), bf16[64,2,160]{2,1,0:T(2,128)(2,1)S(1)}, u32[]{:S(2)}, u32[]{:S(2)}) %all-to-all-start.1) | async-done | bytes 40992 | tf_op jit(solution)/shard_map/all_to_all | solution.py:107
  122.9 0.1 reshape.262
  123.0 0.2 convolution_convert_fusion.4
  123.2 0.8 reshape.263
  124.0 4.4 %all-to-all-start.2 = ((bf16[64,4,160]{2,1,0:T(4,128)(2,1)}), bf16[64,4,160]{2,1,0:T(4,128)(2,1)S(1)}, u32[]{:S(2)}, u32[]{:S(2)}) async-start(bf16[64,4,160]{2,1,0:T(4,128)(2,1)} %reshape.263), calls=%async_computation.2 | async-start | bytes 262144 | tf_op jit(solution)/shard_map/all_to_all | solution.py:116
  133.4 5.5 %all-to-all-done.2 = bf16[64,4,160]{2,1,0:T(4,128)(2,1)S(1)} async-done(((bf16[64,4,160]{2,1,0:T(4,128)(2,1)}), bf16[64,4,160]{2,1,0:T(4,128)(2,1)S(1)}, u32[]{:S(2)}, u32[]{:S(2)}) %all-to-all-start.2) | async-done | bytes 81952 | tf_op jit(solution)/shard_map/all_to_all | solution.py:116
  138.9 0.1 reshape.264
  139.0 0.9 convolution_convert_fusion.3
  (10 shorter events, 0.1 us)
Async XLA Ops:
  6.5 93.4 %copy-start = (bf16[160,5120]{1,0:T(8,128)(2,1)S(1)}, bf16[160,5120]{1,0:T(8,128)(2,1)}, u32[]{:S(2)}) copy-start(bf16[160,5120]{1,0:T(8,128)(2,1)} %param.15) | copy-start | bytes 4915204
  6.5 4.3 %copy-start.2 = (bf16[64,1280]{1,0:T(8,128)(2,1)S(1)}, bf16[64,1280]{1,0:T(8,128)(2,1)}, u32[]{:S(2)}) copy-start(bf16[64,1280]{1,0:T(8,128)(2,1)} %param.12) | copy-start | bytes 491524
  6.5 86.2 %all-gather.2.cloned.1.call-start = ((), (), s32[]{:S(2)}) async-start(), calls=%async_computation.3 | async-start | bytes 3686400 | tf_op jit(solution)/shard_map/all_gather | solution.py:49
  11.5 1.5 %copy-start.1 = (f32[512,1280]{1,0:T(8,128)}, f32[512,1280]{1,0:T(8,128)S(1)}, u32[]{:S(2)}) copy-start(f32[512,1280]{1,0:T(8,128)S(1)} %get-tuple-element.15) | copy-start | bytes 7864324
  11.9 1.8 %copy-start.7 = (bf16[3,160,1280]{2,1,0:T(8,128)(2,1)S(1)}, bf16[3,160,1280]{2,1,0:T(8,128)(2,1)}, u32[]{:S(2)}) copy-start(bf16[3,160,1280]{2,1,0:T(8,128)(2,1)} %param.13) | copy-start | bytes 3686404
  11.9 11.2 %copy-start.3 = (s32[512]{0:T(512)S(1)}, s32[512]{0:T(512)}, u32[]{:S(2)}) copy-start(s32[512]{0:T(512)} %param.16) | copy-start | bytes 6148
  14.3 14.7 %collective-permute-start.2 = (bf16[512,160]{0,1:T(8,128)(2,1)S(1)}, bf16[512,160]{0,1:T(8,128)(2,1)S(1)}, u32[]{:S(2)}, u32[]{:S(2)}) collective-permute-start(bf16[512,160]{0,1:T(8,128)(2,1)S(1)} %convolution_convert_fusion), channel_id=1, source_target_pairs={{0,1},{1,0},{2,3},{3,2},{4,5},{5,4},{6,7},{7,6},{8,9},{9,8},{10,11... | collective-permute-start | bytes 491528 | tf_op jit(solution)/shard_map/ppermute | solution.py:12
  23.1 5.5 %collective-permute-start.1 = (bf16[512]{0:T(512)(128)(2,1)S(1)}, bf16[512]{0:T(512)(128)(2,1)S(1)}, u32[]{:S(2)}, u32[]{:S(2)}) collective-permute-start(bf16[512]{0:T(512)(128)(2,1)S(1)} %get-tuple-element.11), channel_id=1, source_target_pairs={{0,1},{1,0},{2,3},{3,2},{4,5},{5,4},{6,7},{7,6},{8,9},{9,8},{10,11... | collective-permute-start | bytes 3080 | tf_op jit(solution)/shard_map/ppermute | solution.py:12
  25.6 3.4 %collective-permute-start = (bf16[512,160]{0,1:T(8,128)(2,1)S(1)}, bf16[512,160]{0,1:T(8,128)(2,1)S(1)}, u32[]{:S(2)}, u32[]{:S(2)}) collective-permute-start(bf16[512,160]{0,1:T(8,128)(2,1)S(1)} %convolution_convert_fusion.2), channel_id=1, source_target_pairs={{0,1},{1,0},{2,3},{3,2},{4,5},{5,4},{6,7},{7,6},{8,9},{9,8},{10,11... | collective-permute-start | bytes 491528 | tf_op jit(solution)/shard_map/ppermute | solution.py:12
  31.9 5.9 %copy-start.5 = (s32[64]{0:T(128)S(1)}, s32[64]{0:T(128)}, u32[]{:S(2)}) copy-start(s32[64]{0:T(128)} %param.19) | copy-start | bytes 772
  32.0 6.0 %copy-start.4 = (s32[64]{0:T(128)S(1)}, s32[64]{0:T(128)}, u32[]{:S(2)}) copy-start(s32[64]{0:T(128)} %param.18) | copy-start | bytes 772
  32.0 6.0 %copy-start.6 = (s32[64,2]{0,1:T(2,128)S(1)}, s32[64,2]{0,1:T(2,128)}, u32[]{:S(2)}) copy-start(s32[64,2]{0,1:T(2,128)} %param.17) | copy-start | bytes 1540
  33.2 53.2 %all-to-all-start = ((bf16[8,512,160]{1,2,0:T(8,128)(2,1)}), bf16[8,512,160]{1,2,0:T(8,128)(2,1)S(1)}, u32[]{:S(2)}, u32[]{:S(2)}) async-start(bf16[8,512,160]{1,2,0:T(8,128)(2,1)} %broadcast_in_dim.69), calls=%async_computation | async-start | bytes 2621440 | tf_op jit(solution)/shard_map/all_to_all | solution.py:94
  102.7 20.2 %all-to-all-start.1 = ((bf16[64,2,160]{2,1,0:T(2,128)(2,1)}), bf16[64,2,160]{2,1,0:T(2,128)(2,1)S(1)}, u32[]{:S(2)}, u32[]{:S(2)}) async-start(bf16[64,2,160]{2,1,0:T(2,128)(2,1)} %reshape.261), calls=%async_computation.1 | async-start | bytes 131072 | tf_op jit(solution)/shard_map/all_to_all | solution.py:107
  124.0 14.9 %all-to-all-start.2 = ((bf16[64,4,160]{2,1,0:T(4,128)(2,1)}), bf16[64,4,160]{2,1,0:T(4,128)(2,1)S(1)}, u32[]{:S(2)}, u32[]{:S(2)}) async-start(bf16[64,4,160]{2,1,0:T(4,128)(2,1)} %reshape.263), calls=%async_computation.2 | async-start | bytes 262144 | tf_op jit(solution)/shard_map/all_to_all | solution.py:116
Sparse Core Ops, SparseCore 0:
  9.4 83.2 all-gather.1
where the time goes:
time: 147 us
  waiting for transfers between devices  67.3 us (46%)
  starting transfers between devices  32.6 us (22%)
  between operations  21.2 us (14%)
  matrix products  15.1 us (10%)
  local copies, waits for them, and re-layouts  6.95 us (5%)
  other arithmetic  3.64 us (2%)
    all_to_all x1, waiting for transfers between devices, on_device(): gathered = lax.all_to_all(sent, 'head', 0, 0, tiled=True)  44.9 us
    ppermute x3, starting transfers between devices, partner(): lax.ppermute(x, axis, [(i, i ^ 1 << apart) for i in range(lax.axis_size(a...  13.1 us
    all_to_all x1, starting transfers between devices, on_device(): lax.all_to_all(projected.reshape(places, share, width_here), 'tok', 0, 0,...  10.4 us
    all_to_all x1, waiting for transfers between devices, on_device(): lax.all_to_all(projected.reshape(places, share, width_here), 'tok', 0, 0,...  9.7 us
    all_gather x1, waiting for transfers between devices, on_device(): full_weight = lax.all_gather(out_weight, 'head', axis=0, tiled=True)  6.37 us
    all_to_all x1, waiting for transfers between devices, on_device(): lax.all_to_all(pieces.reshape(places, 2 * share, width_here), 'tok', 0, 0...  5.53 us
    dot_general x1, matrix products, on_device(): jnp.einsum('ztf,zfd->td', gathered, full_weight.reshape(group, width_here...  4.83 us
    all_to_all x1, starting transfers between devices, on_device(): gathered = lax.all_to_all(sent, 'head', 0, 0, tiled=True)  4.66 us
  transfers between devices with their start and end apart: 7, of which 4 were waited for; matrix products, arithmetic and copies ran while one was open for 8% of the time, Pallas kernels for 0%

commit v1 on v0

--- a/solution.py
+++ b/solution.py
@@ -6,6 +6,19 @@
 
 HEAD_DIM = 80
 CAP = 248
+
+
+def gather_around(shard, axis, dim):
+    ways = lax.axis_size(axis)
+    up = [(d, (d + 1) % ways) for d in range(ways)]
+    down = [(d, (d - 1) % ways) for d in range(ways)]
+    earlier, later = ([shard], [shard])
+    for _ in range(ways // 2):
+        earlier.append(lax.ppermute(earlier[-1], axis, up))
+    for _ in range((ways - 1) // 2):
+        later.append(lax.ppermute(later[-1], axis, down))
+    line = jnp.concatenate([*earlier[::-1], *later[1:]], axis=dim)
+    return jnp.roll(line, (lax.axis_index(axis) - ways // 2) * shard.shape[dim], axis=dim)
 
 
 def partner(x, axis, apart):
@@ -46,7 +59,7 @@
     image_offsets,
     owners,
 ):
-    full_weight = lax.all_gather(out_weight, "head", axis=0, tiled=True)
+    full_weight = gather_around(out_weight, "head", 0)
     block_rows = patches.shape[0]
     width_here = qkv_weight.shape[1]
     heads_here = width_here // HEAD_DIM

time: 147 us -> 168 us (1.14)
  starting transfers between devices: 32.6 us -> 58.1 us
  local copies, waits for them, and re-layouts: 6.95 us -> 20 us
  between operations: 21.2 us -> 8.17 us
  waiting for transfers between devices: 67.3 us -> 54.7 us
  other arithmetic: 3.64 us -> 6.96 us
  matrix products: 15.1 us -> 18.3 us
    all_to_all x1, waiting for transfers between devices: 44.9 us -> 0.01 us  [on_device(): gathered = lax.all_to_all(sent, 'head', 0, 0, tiled=True)]
    ppermute x0 -> x7, waiting for transfers between devices: none -> 39.6 us  [the longest x3 25.9 us: gather_around(): later.append(lax.ppermute(later[-1], axis, down))]
    ppermute x0 -> x7, starting transfers between devices: none -> 28.6 us  [the longest x3 17.9 us: gather_around(): later.append(lax.ppermute(later[-1], axis, down))]
    unnamed x16 -> x39, local copies, waits for them, and re-layouts: 1.49 us -> 12.1 us
    all_gather x1 -> x0, waiting for transfers between devices: 6.37 us -> none  [on_device(): full_weight = lax.all_gather(out_weight, 'head', axis=0, tiled=True)]
    ppermute x3, starting transfers between devices: 13.1 us -> 7.19 us  [partner(): lax.ppermute(x, axis, [(i, i ^ 1 << apart) for i in range(lax.axis_size(a...]
    all_to_all x1, starting transfers between devices: 10.4 us -> 13.3 us  [on_device(): lax.all_to_all(projected.reshape(places, share, width_here), 'tok', 0, 0,...]
    dynamic_slice x0 -> x1, local copies, waits for them, and re-layouts: none -> 2.45 us  [gather_around(): jnp.roll(line, (lax.axis_index(axis) - ways // 2) * shard.shape[dim], axi...]
  transfers between devices with their start and end apart: 7 -> 13, of which waited for: 4 -> 5; matrix products, arithmetic and copies ran while one was open for 8% -> 19% of each run, Pallas kernels for 0% -> 0%
where the time goes in v1:
time: 168 us; the launch traced here: 166 us
  starting transfers between devices  58.1 us (35%)
  waiting for transfers between devices  54.7 us (33%)
  local copies, waits for them, and re-layouts  20 us (12%)
  matrix products  18.3 us (11%)
  between operations  8.17 us (5%)
  other arithmetic  6.96 us (4%)
    ppermute x3, waiting for transfers between devices, gather_around(): later.append(lax.ppermute(later[-1], axis, down))  25.9 us
    ppermute x3, starting transfers between devices, gather_around(): later.append(lax.ppermute(later[-1], axis, down))  17.9 us
    ppermute x4, waiting for transfers between devices, gather_around(): earlier.append(lax.ppermute(earlier[-1], axis, up))  13.7 us
    all_to_all x1, starting transfers between devices, on_device(): lax.all_to_all(projected.reshape(places, share, width_here), 'tok', 0, 0,...  13.3 us
    unnamed x39, local copies, waits for them, and re-layouts  12.1 us
    ppermute x4, starting transfers between devices, gather_around(): earlier.append(lax.ppermute(earlier[-1], axis, up))  10.7 us
    all_to_all x1, waiting for transfers between devices, on_device(): lax.all_to_all(projected.reshape(places, share, width_here), 'tok', 0, 0,...  9.7 us
    ppermute x3, starting transfers between devices, partner(): lax.ppermute(x, axis, [(i, i ^ 1 << apart) for i in range(lax.axis_size(a...  7.19 us
  transfers between devices with their start and end apart: 13, of which 5 were waited for; matrix products, arithmetic and copies ran while one was open for 19% of the time, Pallas kernels for 0%

profile of v1, /device:TPU:1, one launch (start us, length us, event | category | flops | bytes accessed | tf_op | source)
XLA Modules:
  0.0 166.3 jit_solution(16285843154467064014)
XLA Ops:
  0.0 5.0 %collective-permute-start.3 = (bf16[160,1280]{1,0:T(8,128)(2,1)}, bf16[160,1280]{1,0:T(8,128)(2,1)S(1)}, u32[]{:S(2)}, u32[]{:S(2)}) collective-permute-start(bf16[160,1280]{1,0:T(8,128)(2,1)} %param.14), channel_id=1, source_target_pairs={{0,64},{64,128},{128,192},{192,256},{256,320},{320,384},{384,448},... | collective-permute-start | bytes 1228808 | tf_op jit(solution)/shard_map/ppermute | solution.py:17
  5.0 8.6 %collective-permute-start.7 = (bf16[160,1280]{1,0:T(8,128)(2,1)}, bf16[160,1280]{1,0:T(8,128)(2,1)}, u32[]{:S(2)}, u32[]{:S(2)}) collective-permute-start(bf16[160,1280]{1,0:T(8,128)(2,1)} %param.14), channel_id=1, source_target_pairs={{0,448},{64,0},{128,64},{192,128},{256,192},{320,256},{384,320},{4... | collective-permute-start | bytes 1228808 | tf_op jit(solution)/shard_map/ppermute | solution.py:19
  13.6 0.7 slice_bitcast_fusion
  14.3 0.8 select_reduce_fusion
  15.0 0.1 fusion.22
  15.2 2.0 %convolution_add_fusion.1 = f32[512,1280]{1,0:T(8,128)S(1)} fusion(bf16[64,1280]{1,0:T(8,128)(2,1)} %param.11, bf16[512,1280]{1,0:T(8,128)(2,1)} %param.10, s32[512]{0:T(512)S(1)} %get-tuple-element.13), kind=kOutput, calls=%fused_computation.3 | convolution fusion | flops 85229568 | bytes 4098048 | tf_op jit(solution)/shard_map/dot_general | solution.py:78
  17.2 0.6 fusion.41
  17.8 0.4 multiply_reduce_fusion.1
  18.3 0.3 multiply_convert_fusion.1
  18.6 0.7 copy-done.1
  19.3 0.7 copy-done.11
  20.0 1.2 convolution_convert_fusion
  21.3 2.9 %collective-permute-start.2 = (bf16[512,160]{0,1:T(8,128)(2,1)}, bf16[512,160]{0,1:T(8,128)(2,1)}, u32[]{:S(2)}, u32[]{:S(2)}) collective-permute-start(bf16[512,160]{0,1:T(8,128)(2,1)} %convolution_convert_fusion), channel_id=1, source_target_pairs={{0,1},{1,0},{2,3},{3,2},{4,5},{5,4},{6,7},{7,6},{8,9},{9,8},{10,11... | collective-permute-start | bytes 491528 | tf_op jit(solution)/shard_map/ppermute | solution.py:25
  24.2 1.9 %collective-permute-start.1 = (bf16[512]{0:T(512)(128)(2,1)S(1)}, bf16[512]{0:T(512)(128)(2,1)}, u32[]{:S(2)}, u32[]{:S(2)}) collective-permute-start(bf16[512]{0:T(512)(128)(2,1)S(1)} %get-tuple-element.11), channel_id=1, source_target_pairs={{0,1},{1,0},{2,3},{3,2},{4,5},{5,4},{6,7},{7,6},{8,9},{9,8},{10,11... | collective-permute-start | bytes 3080 | tf_op jit(solution)/shard_map/ppermute | solution.py:25
  26.1 0.6 convolution_convert_fusion.2
  26.7 2.4 %collective-permute-start = (bf16[512,160]{0,1:T(8,128)(2,1)S(1)}, bf16[512,160]{0,1:T(8,128)(2,1)}, u32[]{:S(2)}, u32[]{:S(2)}) collective-permute-start(bf16[512,160]{0,1:T(8,128)(2,1)S(1)} %convolution_convert_fusion.2), channel_id=1, source_target_pairs={{0,1},{1,0},{2,3},{3,2},{4,5},{5,4},{6,7},{7,6},{8,9},{9,8},{10,11... | collective-permute-start | bytes 491528 | tf_op jit(solution)/shard_map/ppermute | solution.py:25
  29.1 0.1 eq.112
  29.2 1.5 fusion.37
  32.7 2.2 %convolution_convert_fusion.1 = bf16[512,160]{0,1:T(8,128)(2,1)} fusion(bf16[512,1280]{1,0:T(8,128)(2,1)S(1)} %multiply_convert_fusion.1, bf16[3,160,1280]{2,1,0:T(8,128)(2,1)} %param.13), kind=kOutput, calls=%fused_computation.14 | convolution fusion | flops 209797120 | bytes 1884160 | tf_op jit(solution)/shard_map/dot_general | solution.py:45
  34.9 0.1 copy.12
  35.7 1.9 %collective-permute-start.4 = (bf16[160,1280]{1,0:T(8,128)(2,1)S(1)}, bf16[160,1280]{1,0:T(8,128)(2,1)S(1)}, u32[]{:S(2)}, u32[]{:S(2)}) collective-permute-start(bf16[160,1280]{1,0:T(8,128)(2,1)S(1)} %collective-permute-done.3), channel_id=1, source_target_pairs={{0,64},{64,128},{128,192},{192,256},{256,320},{320,384},{384,448},... | collective-permute-start | bytes 1228808 | tf_op jit(solution)/shard_map/ppermute | solution.py:17
  37.6 0.7 maximum_convert_fusion
  38.3 0.4 broadcast_compare_fusion
  38.7 1.0 pad_maximum_fusion.1
  39.7 10.2 %collective-permute-done.4 = bf16[160,1280]{1,0:T(8,128)(2,1)S(1)} collective-permute-done((bf16[160,1280]{1,0:T(8,128)(2,1)S(1)}, bf16[160,1280]{1,0:T(8,128)(2,1)S(1)}, u32[]{:S(2)}, u32[]{:S(2)}) %collective-permute-start.4) | collective-permute-done | bytes 409632 | tf_op jit(solution)/shard_map/ppermute | solution.py:17
  49.9 1.9 %collective-permute-start.5 = (bf16[160,1280]{1,0:T(8,128)(2,1)S(1)}, bf16[160,1280]{1,0:T(8,128)(2,1)}, u32[]{:S(2)}, u32[]{:S(2)}) collective-permute-start(bf16[160,1280]{1,0:T(8,128)(2,1)S(1)} %collective-permute-done.4), channel_id=1, source_target_pairs={{0,64},{64,128},{128,192},{192,256},{256,320},{320,384},{384,448},... | collective-permute-start | bytes 1228808 | tf_op jit(solution)/shard_map/ppermute | solution.py:17
  51.8 0.9 pad_maximum_fusion
  52.8 2.4 %fusion = (f32[2,512]{1,0:T(2,128)S(1)}, f32[2,512,1024]{2,1,0:T(8,128)S(1)}) fusion(pred[512,1024]{1,0:T(8,128)(4,1)S(1)} %broadcast_compare_fusion, bf16[512,2,80]{0,2,1:T(8,128)(2,1)} %bitcast.49, bf16[1024,2,80]{0,2,1:T(8,128)(2,1)S(1)} %bitcast.47), kind=kOutput, calls=%fused_computation.4 | convolution fusion | flops 170916864 | bytes 5214208 | tf_op jit(solution)/shard_map/qhd,khd->hqk/dot_general | solution.py:96
  55.2 4.6 %collective-permute-start.8 = (bf16[160,1280]{1,0:T(8,128)(2,1)}, bf16[160,1280]{1,0:T(8,128)(2,1)}, u32[]{:S(2)}, u32[]{:S(2)}) collective-permute-start(bf16[160,1280]{1,0:T(8,128)(2,1)} %collective-permute-done.7), channel_id=1, source_target_pairs={{0,448},{64,0},{128,64},{192,128},{256,192},{320,256},{384,320},{4... | collective-permute-start | bytes 1228808 | tf_op jit(solution)/shard_map/ppermute | solution.py:19
  59.8 3.5 %collective-permute-done.5 = bf16[160,1280]{1,0:T(8,128)(2,1)} collective-permute-done((bf16[160,1280]{1,0:T(8,128)(2,1)S(1)}, bf16[160,1280]{1,0:T(8,128)(2,1)}, u32[]{:S(2)}, u32[]{:S(2)}) %collective-permute-start.5) | collective-permute-done | bytes 409632 | tf_op jit(solution)/shard_map/ppermute | solution.py:17
  63.3 1.9 %collective-permute-start.6 = (bf16[160,1280]{1,0:T(8,128)(2,1)}, bf16[160,1280]{1,0:T(8,128)(2,1)}, u32[]{:S(2)}, u32[]{:S(2)}) collective-permute-start(bf16[160,1280]{1,0:T(8,128)(2,1)} %collective-permute-done.5), channel_id=1, source_target_pairs={{0,64},{64,128},{128,192},{192,256},{256,320},{320,384},{384,448},... | collective-permute-start | bytes 1228808 | tf_op jit(solution)/shard_map/ppermute | solution.py:17
  65.2 1.4 fusion.3
  66.6 1.2 broadcast_in_dim.69
  67.8 4.6 %all-to-all-start = ((bf16[8,512,160]{1,2,0:T(8,128)(2,1)}), bf16[8,512,160]{1,2,0:T(8,128)(2,1)S(1)}, u32[]{:S(2)}, u32[]{:S(2)}) async-start(bf16[8,512,160]{1,2,0:T(8,128)(2,1)} %broadcast_in_dim.69), calls=%async_computation | async-start | bytes 2621440 | tf_op jit(solution)/shard_map/all_to_all | solution.py:107
  72.4 4.7 %collective-permute-start.9 = (bf16[160,1280]{1,0:T(8,128)(2,1)}, bf16[160,1280]{1,0:T(8,128)(2,1)S(1)}, u32[]{:S(2)}, u32[]{:S(2)}) collective-permute-start(bf16[160,1280]{1,0:T(8,128)(2,1)} %collective-permute-done.8), channel_id=1, source_target_pairs={{0,448},{64,0},{128,64},{192,128},{256,192},{320,256},{384,320},{4... | collective-permute-start | bytes 1228808 | tf_op jit(solution)/shard_map/ppermute | solution.py:19
  77.2 1.0 constant_dynamic-update-slice_fusion.15
  78.2 1.0 constant_dynamic-update-slice_fusion.14
  79.3 1.1 constant_dynamic-update-slice_fusion.13
  80.4 1.1 constant_dynamic-update-slice_fusion.12
  81.5 1.0 constant_dynamic-update-slice_fusion.10
  82.5 1.0 constant_dynamic-update-slice_fusion.9
  83.6 25.9 %collective-permute-done.9 = bf16[160,1280]{1,0:T(8,128)(2,1)S(1)} collective-permute-done((bf16[160,1280]{1,0:T(8,128)(2,1)}, bf16[160,1280]{1,0:T(8,128)(2,1)S(1)}, u32[]{:S(2)}, u32[]{:S(2)}) %collective-permute-start.9) | collective-permute-done | bytes 409632 | tf_op jit(solution)/shard_map/ppermute | solution.py:19
  109.5 1.0 constant_dynamic-update-slice_fusion.7
  110.5 1.0 constant_dynamic-update-slice_fusion.6
  111.7 1.0 constant_dynamic-update-slice_fusion.2
  112.7 1.0 constant_dynamic-update-slice_fusion.1
  113.8 2.5 %constant_dynamic-slice_fusion = bf16[1280,1280]{1,0:T(8,128)(2,1)} fusion(bf16[2560,1280]{1,0:T(8,128)(2,1)S(1)} %constant_dynamic-update-slice_fusion, s32[]{:T(128)S(6)} %select_n.174), kind=kLoop, calls=%fused_computation.125 | loop fusion | bytes 6553604 | tf_op jit(solution)/shard_map/jit(_roll_dynamic)/dynamic_slice | solution.py:21
  116.2 4.8 %fusion.42 = (f32[512]{0:T(512)S(1)}, f32[512,1280]{1,0:T(8,128)S(1)}) fusion(f32[512,1280]{1,0:T(8,128)} %copy-done.1, bf16[8,512,160]{1,2,0:T(8,128)(2,1)S(1)} %all-to-all-done, bf16[8,160,1280]{2,1,0:T(8,128)(2,1)} %bitcast.45), kind=kOutput, calls=%fused_computation.130 | convolution fusion | flops 1679031808 | bytes 9832448 | tf_op jit(solution)/shard_map/ztf,zfd->td/dot_general | solution.py:108
  121.1 0.4 multiply_reduce_fusion
  121.5 0.3 multiply_convert_fusion
  121.8 1.7 %reshape.260 = bf16[128,5120]{1,0:T(8,128)(2,1)} reshape(bf16[512,1280]{1,0:T(8,128)(2,1)S(1)} %multiply_convert_fusion) | data formatting | bytes 2621440 | tf_op jit(solution)/shard_map/reshape | solution.py:115
  123.5 1.9 %convolution_convert_fusion.5 = bf16[128,160]{0,1:T(8,128)(2,1)S(1)} fusion(bf16[128,5120]{1,0:T(8,128)(2,1)} %reshape.260, bf16[160,5120]{1,0:T(8,128)(2,1)S(1)} %copy-done), kind=kOutput, calls=%fused_computation.18 | convolution fusion | flops 209735680 | bytes 2990080 | tf_op jit(solution)/shard_map/dot_general | solution.py:45
  125.4 0.1 copy.13
  125.5 0.7 reshape.261
  126.2 13.3 %all-to-all-start.1 = ((bf16[64,2,160]{2,1,0:T(2,128)(2,1)}), bf16[64,2,160]{2,1,0:T(2,128)(2,1)S(1)}, u32[]{:S(2)}, u32[]{:S(2)}) async-start(bf16[64,2,160]{2,1,0:T(2,128)(2,1)} %reshape.261), calls=%async_computation.1 | async-start | bytes 131072 | tf_op jit(solution)/shard_map/all_to_all | solution.py:120
  139.4 0.1 fusion.16
  139.5 9.7 %all-to-all-done.1 = bf16[64,2,160]{2,1,0:T(2,128)(2,1)S(1)} async-done(((bf16[64,2,160]{2,1,0:T(2,128)(2,1)}), bf16[64,2,160]{2,1,0:T(2,128)(2,1)S(1)}, u32[]{:S(2)}, u32[]{:S(2)}) %all-to-all-start.1) | async-done | bytes 40992 | tf_op jit(solution)/shard_map/all_to_all | solution.py:120
  149.2 0.1 reshape.262
  149.3 0.2 convolution_convert_fusion.4
  149.6 0.8 reshape.263
  150.3 4.4 %all-to-all-start.2 = ((bf16[64,4,160]{2,1,0:T(4,128)(2,1)}), bf16[64,4,160]{2,1,0:T(4,128)(2,1)S(1)}, u32[]{:S(2)}, u32[]{:S(2)}) async-start(bf16[64,4,160]{2,1,0:T(4,128)(2,1)} %reshape.263), calls=%async_computation.2 | async-start | bytes 262144 | tf_op jit(solution)/shard_map/all_to_all | solution.py:129
  159.8 5.4 %all-to-all-done.2 = bf16[64,4,160]{2,1,0:T(4,128)(2,1)S(1)} async-done(((bf16[64,4,160]{2,1,0:T(4,128)(2,1)}), bf16[64,4,160]{2,1,0:T(4,128)(2,1)S(1)}, u32[]{:S(2)}, u32[]{:S(2)}) %all-to-all-start.2) | async-done | bytes 81952 | tf_op jit(solution)/shard_map/all_to_all | solution.py:129
  165.3 0.1 reshape.264
  165.3 0.9 convolution_convert_fusion.3
  (43 shorter events, 0.3 us)
Async XLA Ops:
  0.0 123.5 %copy-start = (bf16[160,5120]{1,0:T(8,128)(2,1)S(1)}, bf16[160,5120]{1,0:T(8,128)(2,1)}, u32[]{:S(2)}) copy-start(bf16[160,5120]{1,0:T(8,128)(2,1)} %param.15) | copy-start | bytes 4915204
  0.0 17.2 %copy-start.7 = (bf16[64,1280]{1,0:T(8,128)(2,1)S(1)}, bf16[64,1280]{1,0:T(8,128)(2,1)}, u32[]{:S(2)}) copy-start(bf16[64,1280]{1,0:T(8,128)(2,1)} %param.12) | copy-start | bytes 491524
  0.0 35.7 %collective-permute-start.3 = (bf16[160,1280]{1,0:T(8,128)(2,1)}, bf16[160,1280]{1,0:T(8,128)(2,1)S(1)}, u32[]{:S(2)}, u32[]{:S(2)}) collective-permute-start(bf16[160,1280]{1,0:T(8,128)(2,1)} %param.14), channel_id=1, source_target_pairs={{0,64},{64,128},{128,192},{192,256},{256,320},{320,384},{384,448},... | collective-permute-start | bytes 1228808 | tf_op jit(solution)/shard_map/ppermute | solution.py:17
  5.0 50.2 %collective-permute-start.7 = (bf16[160,1280]{1,0:T(8,128)(2,1)}, bf16[160,1280]{1,0:T(8,128)(2,1)}, u32[]{:S(2)}, u32[]{:S(2)}) collective-permute-start(bf16[160,1280]{1,0:T(8,128)(2,1)} %param.14), channel_id=1, source_target_pairs={{0,448},{64,0},{128,64},{192,128},{256,192},{320,256},{384,320},{4... | collective-permute-start | bytes 1228808 | tf_op jit(solution)/shard_map/ppermute | solution.py:19
  17.8 1.5 copy-start.1
  17.8 2.2 %copy-start.11 = (bf16[3,160,1280]{2,1,0:T(8,128)(2,1)S(1)}, bf16[3,160,1280]{2,1,0:T(8,128)(2,1)}, u32[]{:S(2)}) copy-start(bf16[3,160,1280]{2,1,0:T(8,128)(2,1)} %param.13) | copy-start | bytes 3686404
  18.2 5.9 %copy-start.8 = (s32[512]{0:T(512)S(1)}, s32[512]{0:T(512)}, u32[]{:S(2)}) copy-start(s32[512]{0:T(512)} %param.16) | copy-start | bytes 6148
  18.3 10.9 %copy-start.10 = (s32[64]{0:T(128)S(1)}, s32[64]{0:T(128)}, u32[]{:S(2)}) copy-start(s32[64]{0:T(128)} %param.19) | copy-start | bytes 772
  18.3 11.0 %copy-start.9 = (s32[64]{0:T(128)S(1)}, s32[64]{0:T(128)}, u32[]{:S(2)}) copy-start(s32[64]{0:T(128)} %param.18) | copy-start | bytes 772
  21.3 17.4 %collective-permute-start.2 = (bf16[512,160]{0,1:T(8,128)(2,1)}, bf16[512,160]{0,1:T(8,128)(2,1)}, u32[]{:S(2)}, u32[]{:S(2)}) collective-permute-start(bf16[512,160]{0,1:T(8,128)(2,1)} %convolution_convert_fusion), channel_id=1, source_target_pairs={{0,1},{1,0},{2,3},{3,2},{4,5},{5,4},{6,7},{7,6},{8,9},{9,8},{10,11... | collective-permute-start | bytes 491528 | tf_op jit(solution)/shard_map/ppermute | solution.py:25
  24.2 13.5 %collective-permute-start.1 = (bf16[512]{0:T(512)(128)(2,1)S(1)}, bf16[512]{0:T(512)(128)(2,1)}, u32[]{:S(2)}, u32[]{:S(2)}) collective-permute-start(bf16[512]{0:T(512)(128)(2,1)S(1)} %get-tuple-element.11), channel_id=1, source_target_pairs={{0,1},{1,0},{2,3},{3,2},{4,5},{5,4},{6,7},{7,6},{8,9},{9,8},{10,11... | collective-permute-start | bytes 3080 | tf_op jit(solution)/shard_map/ppermute | solution.py:25
  26.7 25.1 %collective-permute-start = (bf16[512,160]{0,1:T(8,128)(2,1)S(1)}, bf16[512,160]{0,1:T(8,128)(2,1)}, u32[]{:S(2)}, u32[]{:S(2)}) collective-permute-start(bf16[512,160]{0,1:T(8,128)(2,1)S(1)} %convolution_convert_fusion.2), channel_id=1, source_target_pairs={{0,1},{1,0},{2,3},{3,2},{4,5},{5,4},{6,7},{7,6},{8,9},{9,8},{10,11... | collective-permute-start | bytes 491528 | tf_op jit(solution)/shard_map/ppermute | solution.py:25
  35.7 19.5 %copy-start.3 = (bf16[160,1280]{1,0:T(8,128)(2,1)}, bf16[160,1280]{1,0:T(8,128)(2,1)S(1)}, u32[]{:S(2)}) copy-start(bf16[160,1280]{1,0:T(8,128)(2,1)S(1)} %collective-permute-done.3) | copy-start | bytes 1228804
  35.7 14.2 %collective-permute-start.4 = (bf16[160,1280]{1,0:T(8,128)(2,1)S(1)}, bf16[160,1280]{1,0:T(8,128)(2,1)S(1)}, u32[]{:S(2)}, u32[]{:S(2)}) collective-permute-start(bf16[160,1280]{1,0:T(8,128)(2,1)S(1)} %collective-permute-done.3), channel_id=1, source_target_pairs={{0,64},{64,128},{128,192},{192,256},{256,320},{320,384},{384,448},... | collective-permute-start | bytes 1228808 | tf_op jit(solution)/shard_map/ppermute | solution.py:17
  49.9 5.3 %copy-start.5 = (bf16[160,1280]{1,0:T(8,128)(2,1)}, bf16[160,1280]{1,0:T(8,128)(2,1)S(1)}, u32[]{:S(2)}) copy-start(bf16[160,1280]{1,0:T(8,128)(2,1)S(1)} %collective-permute-done.4) | copy-start | bytes 1228804
  49.9 13.4 %collective-permute-start.5 = (bf16[160,1280]{1,0:T(8,128)(2,1)S(1)}, bf16[160,1280]{1,0:T(8,128)(2,1)}, u32[]{:S(2)}, u32[]{:S(2)}) collective-permute-start(bf16[160,1280]{1,0:T(8,128)(2,1)S(1)} %collective-permute-done.4), channel_id=1, source_target_pairs={{0,64},{64,128},{128,192},{192,256},{256,320},{320,384},{384,448},... | collective-permute-start | bytes 1228808 | tf_op jit(solution)/shard_map/ppermute | solution.py:17
  55.2 17.2 %collective-permute-start.8 = (bf16[160,1280]{1,0:T(8,128)(2,1)}, bf16[160,1280]{1,0:T(8,128)(2,1)}, u32[]{:S(2)}, u32[]{:S(2)}) collective-permute-start(bf16[160,1280]{1,0:T(8,128)(2,1)} %collective-permute-done.7), channel_id=1, source_target_pairs={{0,448},{64,0},{128,64},{192,128},{256,192},{320,256},{384,320},{4... | collective-permute-start | bytes 1228808 | tf_op jit(solution)/shard_map/ppermute | solution.py:19
  63.3 13.9 %collective-permute-start.6 = (bf16[160,1280]{1,0:T(8,128)(2,1)}, bf16[160,1280]{1,0:T(8,128)(2,1)}, u32[]{:S(2)}, u32[]{:S(2)}) collective-permute-start(bf16[160,1280]{1,0:T(8,128)(2,1)} %collective-permute-done.5), channel_id=1, source_target_pairs={{0,64},{64,128},{128,192},{192,256},{256,320},{320,384},{384,448},... | collective-permute-start | bytes 1228808 | tf_op jit(solution)/shard_map/ppermute | solution.py:17
  67.8 13.7 %copy-start.2 = (bf16[160,1280]{1,0:T(8,128)(2,1)S(1)}, bf16[160,1280]{1,0:T(8,128)(2,1)}, u32[]{:S(2)}) copy-start(bf16[160,1280]{1,0:T(8,128)(2,1)} %param.14) | copy-start | bytes 1228804
  67.8 48.4 %all-to-all-start = ((bf16[8,512,160]{1,2,0:T(8,128)(2,1)}), bf16[8,512,160]{1,2,0:T(8,128)(2,1)S(1)}, u32[]{:S(2)}, u32[]{:S(2)}) async-start(bf16[8,512,160]{1,2,0:T(8,128)(2,1)} %broadcast_in_dim.69), calls=%async_computation | async-start | bytes 2621440 | tf_op jit(solution)/shard_map/all_to_all | solution.py:107
  72.4 37.0 %collective-permute-start.9 = (bf16[160,1280]{1,0:T(8,128)(2,1)}, bf16[160,1280]{1,0:T(8,128)(2,1)S(1)}, u32[]{:S(2)}, u32[]{:S(2)}) collective-permute-start(bf16[160,1280]{1,0:T(8,128)(2,1)} %collective-permute-done.8), channel_id=1, source_target_pairs={{0,448},{64,0},{128,64},{192,128},{256,192},{320,256},{384,320},{4... | collective-permute-start | bytes 1228808 | tf_op jit(solution)/shard_map/ppermute | solution.py:19
  79.2 32.3 %copy-start.6 = (bf16[160,1280]{1,0:T(8,128)(2,1)S(1)}, bf16[160,1280]{1,0:T(8,128)(2,1)}, u32[]{:S(2)}) copy-start(bf16[160,1280]{1,0:T(8,128)(2,1)} %copy-done.5) | copy-start | bytes 1228804
  80.3 31.2 %copy-start.4 = (bf16[160,1280]{1,0:T(8,128)(2,1)S(1)}, bf16[160,1280]{1,0:T(8,128)(2,1)}, u32[]{:S(2)}) copy-start(bf16[160,1280]{1,0:T(8,128)(2,1)} %copy-done.3) | copy-start | bytes 1228804
  126.2 23.1 %all-to-all-start.1 = ((bf16[64,2,160]{2,1,0:T(2,128)(2,1)}), bf16[64,2,160]{2,1,0:T(2,128)(2,1)S(1)}, u32[]{:S(2)}, u32[]{:S(2)}) async-start(bf16[64,2,160]{2,1,0:T(2,128)(2,1)} %reshape.261), calls=%async_computation.1 | async-start | bytes 131072 | tf_op jit(solution)/shard_map/all_to_all | solution.py:120
  150.3 14.9 %all-to-all-start.2 = ((bf16[64,4,160]{2,1,0:T(4,128)(2,1)}), bf16[64,4,160]{2,1,0:T(4,128)(2,1)S(1)}, u32[]{:S(2)}, u32[]{:S(2)}) async-start(bf16[64,4,160]{2,1,0:T(4,128)(2,1)} %reshape.263), calls=%async_computation.2 | async-start | bytes 262144 | tf_op jit(solution)/shard_map/all_to_all | solution.py:129
